TPU v7x, 32 devices: a whole 2x2x4 slice. The times are simulated.
32 devices in a mesh: light: 4 (over x, core), strip: 8 (over z, y).
Axes of the slice: x: 2, y: 2, z: 4, core: 2. Of those that a mesh axis runs over, the one named last changes fastest.
Arguments:
- depth_start: float32 [128, 4096], P(None, 'strip'), may hold values from -0.3 to 0.3
- albedo_start: float32 [128, 4096], P(None, 'strip'), may hold values from 0.5 to 2
- observations: bfloat16 [32, 128, 4096], P('light', None, 'strip'), may hold values from 0 to 26
- light_table: int32 [32, 4], P('light'), may hold values from 0 to 999
- valid_mask: int32 [128, 4096], P(None, 'strip'), may hold values 0 or 1
Outputs:
- depth_final: float32 [128, 4096], P(None, 'strip')
- albedo_final: float32 [128, 4096], P(None, 'strip')
All inputs are finite; a program needn't handle non-finite values. No bound on the sum of `valid_mask` on one device may be relied on, other than what follows from the above.
Results may differ from a plain program's by a relative error of at most 0.0003.
Values may be sent and summed in bfloat16 or wider, within the bound.
No kernel may reach another device: no remote copies, remote signals or barrier semaphores. Data moves between devices by JAX's collectives and lax.ppermute only.
A program may use at most 64 MiB of HBM per device.

v0:
```python
import jax
import jax.numpy as jnp
from jax import lax
from jax.sharding import PartitionSpec as P

ITERS = 2
temper = 0.5
step_depth = 0.1
step_albedo = 0.2
epsilon = 1e-06


def extended(block, sides, width):
    for axis, dim in sides:
        count = lax.axis_size(axis)
        forward = [(i, i + 1) for i in range(count - 1)]
        backward = [(target, source) for source, target in forward]
        low = lax.ppermute(
            lax.slice_in_dim(block, block.shape[dim] - width, None, axis=dim), axis, forward
        )
        high = lax.ppermute(lax.slice_in_dim(block, 0, width, axis=dim), axis, backward)
        block = jnp.concatenate([low, block, high], axis=dim)
    return block


def decode_lights(table):
    values = table.astype(jnp.float32)
    light_x = (values[:, 0] / 500.0 - 1.0)[:, None, None]
    light_y = (values[:, 1] / 500.0 - 1.0)[:, None, None]
    light_z = (1.0 + values[:, 2] / 1000.0)[:, None, None]
    intensity = (0.5 + values[:, 3] / 1000.0)[:, None, None]
    return (light_x, light_y, light_z, intensity)


def shade_terms(surface, col_pad, row_pad, albedo, observed, table, valid, coord_x, coord_y):
    slope_x = 0.5 * (col_pad[:, 2:] - col_pad[:, :-2])
    slope_y = 0.5 * (row_pad[2:] - row_pad[:-2])
    light_x, light_y, light_z, intensity = decode_lights(table)
    delta_x = light_x - coord_x
    delta_y = light_y - coord_y
    delta_z = light_z - surface
    distance_sq = delta_x * delta_x + delta_y * delta_y + delta_z * delta_z
    norm_sq = 1.0 + slope_x * slope_x + slope_y * slope_y
    facing = -slope_x * delta_x - slope_y * delta_y + delta_z
    falloff = intensity / (distance_sq * jnp.sqrt(distance_sq) * jnp.sqrt(norm_sq))
    radiance = albedo * falloff * facing
    residual = valid * (radiance - observed.astype(jnp.float32))
    scores = -temper * residual * residual
    return (
        scores,
        residual,
        falloff,
        facing,
        delta_x,
        delta_y,
        delta_z,
        distance_sq,
        norm_sq,
        slope_x,
        slope_y,
    )


def light_gradients(weights, terms, albedo):
    (
        scores,
        residual,
        falloff,
        facing,
        delta_x,
        delta_y,
        delta_z,
        distance_sq,
        norm_sq,
        slope_x,
        slope_y,
    ) = terms
    lit = weights * residual * falloff
    grad_albedo = jnp.sum(lit * facing, axis=0)
    scaled = lit * albedo
    grad_direct = jnp.sum(scaled * (-1.0 + 3.0 * facing * delta_z / distance_sq), axis=0)
    grad_x = jnp.sum(scaled * (-delta_x - facing * slope_x / norm_sq), axis=0)
    grad_y = jnp.sum(scaled * (-delta_y - facing * slope_y / norm_sq), axis=0)
    return (grad_x, grad_y, grad_direct, grad_albedo)


def depth_stencil(grad_x_pad, grad_y_pad, grad_direct):
    return (
        grad_direct
        + 0.5 * (grad_x_pad[:, :-2] - grad_x_pad[:, 2:])
        + 0.5 * (grad_y_pad[:-2] - grad_y_pad[2:])
    )


def coordinates(nrows, total_rows, strip_cols):
    total_cols = strip_cols * lax.axis_size("strip")
    col_start = lax.axis_index("strip") * strip_cols
    columns = (jnp.arange(strip_cols) + col_start).astype(jnp.float32)
    coord_x = ((columns + 0.5) / total_cols - 0.5)[None, :]
    row_index = jnp.arange(nrows).astype(jnp.float32)
    coord_y = ((row_index + 0.5 - total_rows / 2.0) / total_cols)[:, None]
    return (coord_x, coord_y)


def update(surface, albedo, full_depth, full_albedo, mean_depth, mean_albedo):
    surface = surface - step_depth * jnp.tanh(full_depth / jnp.sqrt(mean_depth + epsilon))
    albedo = albedo - step_albedo * jnp.tanh(full_albedo / jnp.sqrt(mean_albedo + epsilon))
    return (surface, albedo)


def shards(depth_start, albedo_start, observations, light_table, valid_mask):
    strip_cols = depth_start.shape[1]
    total_rows = depth_start.shape[0]
    surface = depth_start
    albedo = albedo_start
    valid = valid_mask.astype(jnp.float32)
    coord_x, coord_y = coordinates(total_rows, total_rows, strip_cols)
    for iteration in range(ITERS):
        col_pad = extended(surface, (("strip", 1),), 1)
        row_pad = jnp.pad(surface, ((1, 1), (0, 0)))
        terms = shade_terms(
            surface, col_pad, row_pad, albedo, observations, light_table, valid, coord_x, coord_y
        )
        scores = terms[0]
        local_high = jnp.max(scores, axis=0)
        highest = lax.pmax(local_high, "light")
        raised = jnp.exp(scores - highest)
        summed = lax.psum(jnp.sum(raised, axis=0), "light")
        weights = raised / summed
        grad_x, grad_y, grad_direct, grad_albedo = light_gradients(weights, terms, albedo)
        grad_x, grad_y, grad_direct, full_albedo = lax.psum(
            (grad_x, grad_y, grad_direct, grad_albedo), "light"
        )
        slope_pad = extended(grad_x, (("strip", 1),), 1)
        full_depth = depth_stencil(slope_pad, jnp.pad(grad_y, ((1, 1), (0, 0))), grad_direct)
        square_depth, square_albedo = lax.psum(
            (jnp.sum(full_depth * full_depth), jnp.sum(full_albedo * full_albedo)), "strip"
        )
        pixel_count = full_depth.size * lax.axis_size("strip")
        surface, albedo = update(
            surface,
            albedo,
            full_depth,
            full_albedo,
            square_depth / pixel_count,
            square_albedo / pixel_count,
        )
    return (surface, albedo)


def solution(mesh):
    in_specs = (
        P(None, "strip"),
        P(None, "strip"),
        P("light", None, "strip"),
        P("light", None),
        P(None, "strip"),
    )
    out_specs = (P(None, "strip"), P(None, "strip"))
    return jax.shard_map(shards, mesh=mesh, in_specs=in_specs, out_specs=out_specs, check_vma=False)
```

profile of v0, /device:TPU:0, one launch (start us, length us, event | category | flops | bytes accessed | tf_op | source)
XLA Modules:
  0.0 334.7 jit_solution(5058168484332134036)
XLA Ops:
  9.6 5.5 %collective-permute-start.1 = (f32[128,1]{1,0:T(8,128)S(1)}, f32[128,1]{1,0:T(8,128)S(1)}, u32[]{:S(2)}, u32[]{:S(2)}) collective-permute-start(f32[128,1]{1,0:T(8,128)S(1)} %get-tuple-element.45), channel_id=1, source_target_pairs={{0,1},{1,2},{2,3},{3,4},{4,5},{5,6},{6,7},{8,9},{9,10},{10,11},{11... | collective-permute-start | bytes 1544 | tf_op jit(solution)/shard_map/ppermute | solution.py:18
  17.1 2.3 fusion.45
  20.2 2.7 fusion.15
  23.0 35.8 %all-reduce.15.cloned.1.call-done = f32[128,512]{1,0:T(8,128)} async-done(((f32[128,512]{1,0:T(8,128)}), f32[128,512]{1,0:T(8,128)}) %all-reduce.15.cloned.1.call-update) | async-done | bytes 262160 | tf_op jit(solution)/shard_map/pmax | solution.py:126
  58.9 2.1 fusion.14
  61.0 32.5 %all-reduce.17.cloned.1.call-done = f32[128,512]{1,0:T(8,128)} async-done(((f32[128,512]{1,0:T(8,128)}), f32[128,512]{1,0:T(8,128)}) %all-reduce.17.cloned.1.call-update) | async-done | bytes 262160 | tf_op jit(solution)/shard_map/psum | solution.py:128
  93.5 5.8 %multiply_reduce_fusion.5 = (f32[128,512]{1,0:T(8,128)}, f32[128,512]{1,0:T(8,128)}, f32[128,512]{1,0:T(8,128)}, f32[128,512]{1,0:T(8,128)}) fusion(f32[128,512]{1,0:T(8,128)} %get-tuple-element.35, f32[128,512]{1,0:T(8,128)} %copy-done.15, f32[8,512]{1,0:T(8,128)S(1)} %get-tuple-element.46, f32[8,128]{1,0:T(8,128)S(1)} %get-tuple-element.55, ...), kind=kLoop, calls=%fused_computation.33 | loop fusion | flops 18612224 | bytes 5566528 | tf_op jit(solution)/shard_map/reduce_sum | solution.py:82
  99.4 36.6 %all-reduce.25.cloned.1.call-done = (f32[128,512]{1,0:T(8,128)}, f32[128,512]{1,0:T(8,128)}, f32[128,512]{1,0:T(8,128)}, f32[128,512]{1,0:T(8,128)}) async-done(((f32[128,512]{1,0:T(8,128)}, f32[128,512]{1,0:T(8,128)}, f32[128,512]{1,0:T(8,128)}, f32[128,512]{1,0:T(8,128)}), (f32[128,512]{1,0:T(8,128)}, f32[128,512]{1,0:T(8,128)}, f32[128,512]{1,0:T(8,128)}, ...) | async-done | bytes 1048592 | tf_op jit(solution)/shard_map/psum | solution.py:131
  136.9 3.4 %collective-permute-start.2 = (f32[128,1]{1,0:T(8,128)S(1)}, f32[128,1]{1,0:T(8,128)S(1)}, u32[]{:S(2)}, u32[]{:S(2)}) collective-permute-start(f32[128,1]{1,0:T(8,128)S(1)} %get-tuple-element.42), channel_id=1, source_target_pairs={{0,1},{1,2},{2,3},{3,4},{4,5},{5,6},{6,7},{8,9},{9,10},{10,11},{11... | collective-permute-start | bytes 1544 | tf_op jit(solution)/shard_map/ppermute | solution.py:18
  143.2 3.2 collective-permute-done.3
  146.5 2.1 multiply_reduce_fusion.9
  148.6 20.2 %all-reduce.5 = (f32[]{:T(128)}, f32[]{:T(128)}) all-reduce(f32[]{:T(128)} %get-tuple-element.30, f32[]{:T(128)} %multiply_reduce_fusion.8), channel_id=1, replica_groups=mesh['light'=4,'strip'=8] {'strip'}, use_global_device_ids=true, to_apply=%region_11.12 | all-reduce | flops 2 | bytes 16 | tf_op jit(solution)/shard_map/psum | solution.py:136
  171.6 4.5 %collective-permute-start.5 = (f32[128,1]{1,0:T(8,128)S(1)}, f32[128,1]{1,0:T(8,128)S(1)}, u32[]{:S(2)}, u32[]{:S(2)}) collective-permute-start(f32[128,1]{1,0:T(8,128)S(1)} %get-tuple-element.41), channel_id=1, source_target_pairs={{0,1},{1,2},{2,3},{3,4},{4,5},{5,6},{6,7},{8,9},{9,10},{10,11},{11... | collective-permute-start | bytes 1544 | tf_op jit(solution)/shard_map/ppermute | solution.py:18
  179.7 4.0 %fusion.17 = (f32[128,512]{1,0:T(8,128)}, f32[8,128,512]{2,1,0:T(8,128)S(1)}) fusion(bf16[8,128,512]{2,1,0:T(8,128)(2,1)} %param.7, f32[8,128]{1,0:T(8,128)S(1)} %get-tuple-element.55, f32[128,512]{1,0:T(8,128)S(1)} %get-tuple-element.29, f32[8,512]{1,0:T(8,128)S(1)} %get-tuple-element.48, f32[128,512]{1,0:T(8,128)S(1)} %neg.27, ...), kind=kLoop, calls=%fused_computation.41 | loop fusion | flops 9895936 | bytes 5021760 | tf_op jit(solution)/shard_map/reduce_max | solution.py:125
  183.7 31.2 %all-reduce.19.cloned.1.call-done = f32[128,512]{1,0:T(8,128)} async-done(((f32[128,512]{1,0:T(8,128)}), f32[128,512]{1,0:T(8,128)}) %all-reduce.19.cloned.1.call-update) | async-done | bytes 262160 | tf_op jit(solution)/shard_map/pmax | solution.py:126
  214.9 2.1 fusion.16
  217.1 32.4 %all-reduce.21.cloned.1.call-done = f32[128,512]{1,0:T(8,128)} async-done(((f32[128,512]{1,0:T(8,128)}), f32[128,512]{1,0:T(8,128)}) %all-reduce.21.cloned.1.call-update) | async-done | bytes 262160 | tf_op jit(solution)/shard_map/psum | solution.py:128
  249.5 5.7 %multiply_reduce_fusion.2 = (f32[128,512]{1,0:T(8,128)}, f32[128,512]{1,0:T(8,128)}, f32[128,512]{1,0:T(8,128)}, f32[128,512]{1,0:T(8,128)}) fusion(f32[128,512]{1,0:T(8,128)} %get-tuple-element.27, f32[128,512]{1,0:T(8,128)} %copy-done.14, f32[128,512]{1,0:T(8,128)S(1)} %copy-done.9, f32[128,512]{1,0:T(8,128)S(1)} %neg.27, ...), kind=kLoop, calls=%fused_computation.28 | loop fusion | flops 18612224 | bytes 5566528 | tf_op jit(solution)/shard_map/reduce_sum | solution.py:82
  255.2 36.6 %all-reduce.23.cloned.1.call-done = (f32[128,512]{1,0:T(8,128)}, f32[128,512]{1,0:T(8,128)}, f32[128,512]{1,0:T(8,128)}, f32[128,512]{1,0:T(8,128)}) async-done(((f32[128,512]{1,0:T(8,128)}, f32[128,512]{1,0:T(8,128)}, f32[128,512]{1,0:T(8,128)}, f32[128,512]{1,0:T(8,128)}), (f32[128,512]{1,0:T(8,128)}, f32[128,512]{1,0:T(8,128)}, f32[128,512]{1,0:T(8,128)}, ...) | async-done | bytes 1048592 | tf_op jit(solution)/shard_map/psum | solution.py:131
  292.8 3.4 %collective-permute-start.6 = (f32[128,1]{1,0:T(8,128)S(1)}, f32[128,1]{1,0:T(8,128)S(1)}, u32[]{:S(2)}, u32[]{:S(2)}) collective-permute-start(f32[128,1]{1,0:T(8,128)S(1)} %get-tuple-element.38), channel_id=1, source_target_pairs={{0,1},{1,2},{2,3},{3,4},{4,5},{5,6},{6,7},{8,9},{9,10},{10,11},{11... | collective-permute-start | bytes 1544 | tf_op jit(solution)/shard_map/ppermute | solution.py:18
  299.1 3.2 collective-permute-done.7
  302.3 2.1 multiply_reduce_fusion.7
  304.4 20.2 %all-reduce.4 = (f32[]{:T(128)}, f32[]{:T(128)}) all-reduce(f32[]{:T(128)} %get-tuple-element.22, f32[]{:T(128)} %multiply_reduce_fusion.6), channel_id=1, replica_groups=mesh['light'=4,'strip'=8] {'strip'}, use_global_device_ids=true, to_apply=%region_27.28 | all-reduce | flops 2 | bytes 16 | tf_op jit(solution)/shard_map/psum | solution.py:136
  326.0 1.8 multiply_subtract_fusion
  (74 shorter events, 18.1 us)
Async XLA Ops:
  7.2 13.0 %copy-start = (f32[128,512]{1,0:T(8,128)S(1)}, f32[128,512]{1,0:T(8,128)}, u32[]{:S(2)}) copy-start(f32[128,512]{1,0:T(8,128)} %param.5) | copy-start | bytes 786436
  7.2 13.0 %copy-start.1 = (bf16[8,128,512]{2,1,0:T(8,128)(2,1)S(1)}, bf16[8,128,512]{2,1,0:T(8,128)(2,1)}, u32[]{:S(2)}) copy-start(bf16[8,128,512]{2,1,0:T(8,128)(2,1)} %param.7) | copy-start | bytes 3145732
  7.2 51.7 %all-reduce.15.cloned.1.call-start = ((), (), s32[]{:S(2)}) async-start(), calls=%async_computation | async-start | bytes 524288 | tf_op jit(solution)/shard_map/pmax | solution.py:126
  8.3 8.7 %collective-permute-start = (f32[128,1]{1,0:T(8,128)S(1)}, f32[128,1]{1,0:T(8,128)S(1)}, u32[]{:S(2)}, u32[]{:S(2)}) collective-permute-start(f32[128,1]{1,0:T(8,128)S(1)} %get-tuple-element.44), channel_id=1, source_target_pairs={{1,0},{2,1},{3,2},{4,3},{5,4},{6,5},{7,6},{9,8},{10,9},{11,10},{12... | collective-permute-start | bytes 1544 | tf_op jit(solution)/shard_map/ppermute | solution.py:21
  9.6 7.6 %collective-permute-start.1 = (f32[128,1]{1,0:T(8,128)S(1)}, f32[128,1]{1,0:T(8,128)S(1)}, u32[]{:S(2)}, u32[]{:S(2)}) collective-permute-start(f32[128,1]{1,0:T(8,128)S(1)} %get-tuple-element.45), channel_id=1, source_target_pairs={{0,1},{1,2},{2,3},{3,4},{4,5},{5,6},{6,7},{8,9},{9,10},{10,11},{11... | collective-permute-start | bytes 1544 | tf_op jit(solution)/shard_map/ppermute | solution.py:18
  17.0 5.9 %copy-start.2 = (f32[128,512]{1,0:T(8,128)}, f32[128,512]{1,0:T(8,128)S(1)}, u32[]{:S(2)}) copy-start(f32[128,512]{1,0:T(8,128)S(1)} %convert_element_type.30) | copy-start | bytes 786436
  22.9 70.6 %copy-start.7 = (f32[128,512]{1,0:T(8,128)S(1)}, f32[128,512]{1,0:T(8,128)}, u32[]{:S(2)}) copy-start(f32[128,512]{1,0:T(8,128)} %param.6) | copy-start | bytes 786436
  22.9 70.6 %copy-start.5 = (f32[128,512]{1,0:T(8,128)S(1)}, f32[128,512]{1,0:T(8,128)}, u32[]{:S(2)}) copy-start(f32[128,512]{1,0:T(8,128)} %copy-done.4) | copy-start | bytes 786436
  22.9 70.6 %copy-start.11 = (f32[128,512]{1,0:T(8,128)S(1)}, f32[128,512]{1,0:T(8,128)}, u32[]{:S(2)}) copy-start(f32[128,512]{1,0:T(8,128)} %copy-done.10) | copy-start | bytes 786436
  23.0 70.5 %copy-start.13 = (f32[128,512]{1,0:T(8,128)S(1)}, f32[128,512]{1,0:T(8,128)}, u32[]{:S(2)}) copy-start(f32[128,512]{1,0:T(8,128)} %copy-done.12) | copy-start | bytes 786436
  23.0 70.5 %all-reduce.17.cloned.1.call-start = ((), (), s32[]{:S(2)}) async-start(), calls=%async_computation.1 | async-start | bytes 524288 | tf_op jit(solution)/shard_map/psum | solution.py:128
  61.0 75.0 %all-reduce.25.cloned.1.call-start = ((), (), s32[]{:S(2)}) async-start(), calls=%async_computation.5 | async-start | bytes 2097152 | tf_op jit(solution)/shard_map/psum | solution.py:131
  99.3 115.6 %all-reduce.19.cloned.1.call-start = ((), (), s32[]{:S(2)}) async-start(), calls=%async_computation.2 | async-start | bytes 524288 | tf_op jit(solution)/shard_map/pmax | solution.py:126
  135.9 40.2 %copy-start.16 = (f32[128,512]{1,0:T(8,128)S(1)}, f32[128,512]{1,0:T(8,128)}, u32[]{:S(2)}) copy-start(f32[128,512]{1,0:T(8,128)} %get-tuple-element.21) | copy-start | bytes 786436
  136.9 6.3 %collective-permute-start.2 = (f32[128,1]{1,0:T(8,128)S(1)}, f32[128,1]{1,0:T(8,128)S(1)}, u32[]{:S(2)}, u32[]{:S(2)}) collective-permute-start(f32[128,1]{1,0:T(8,128)S(1)} %get-tuple-element.42), channel_id=1, source_target_pairs={{0,1},{1,2},{2,3},{3,4},{4,5},{5,6},{6,7},{8,9},{9,10},{10,11},{11... | collective-permute-start | bytes 1544 | tf_op jit(solution)/shard_map/ppermute | solution.py:18
  140.3 6.2 %collective-permute-start.3 = (f32[128,1]{1,0:T(8,128)S(1)}, f32[128,1]{1,0:T(8,128)S(1)}, u32[]{:S(2)}, u32[]{:S(2)}) collective-permute-start(f32[128,1]{1,0:T(8,128)S(1)} %get-tuple-element.43), channel_id=1, source_target_pairs={{1,0},{2,1},{3,2},{4,3},{5,4},{6,5},{7,6},{9,8},{10,9},{11,10},{12... | collective-permute-start | bytes 1544 | tf_op jit(solution)/shard_map/ppermute | solution.py:21
  148.6 31.1 %copy-start.3 = (f32[128,512]{1,0:T(8,128)S(1)}, f32[128,512]{1,0:T(8,128)}, u32[]{:S(2)}) copy-start(f32[128,512]{1,0:T(8,128)} %copy-done.2) | copy-start | bytes 786436
  170.3 6.2 %collective-permute-start.4 = (f32[128,1]{1,0:T(8,128)S(1)}, f32[128,1]{1,0:T(8,128)S(1)}, u32[]{:S(2)}, u32[]{:S(2)}) collective-permute-start(f32[128,1]{1,0:T(8,128)S(1)} %get-tuple-element.40), channel_id=1, source_target_pairs={{1,0},{2,1},{3,2},{4,3},{5,4},{6,5},{7,6},{9,8},{10,9},{11,10},{12... | collective-permute-start | bytes 1544 | tf_op jit(solution)/shard_map/ppermute | solution.py:21
  171.6 6.4 %collective-permute-start.5 = (f32[128,1]{1,0:T(8,128)S(1)}, f32[128,1]{1,0:T(8,128)S(1)}, u32[]{:S(2)}, u32[]{:S(2)}) collective-permute-start(f32[128,1]{1,0:T(8,128)S(1)} %get-tuple-element.41), channel_id=1, source_target_pairs={{0,1},{1,2},{2,3},{3,4},{4,5},{5,6},{6,7},{8,9},{9,10},{10,11},{11... | collective-permute-start | bytes 1544 | tf_op jit(solution)/shard_map/ppermute | solution.py:18
  183.7 65.8 %copy-start.9 = (f32[128,512]{1,0:T(8,128)S(1)}, f32[128,512]{1,0:T(8,128)}, u32[]{:S(2)}) copy-start(f32[128,512]{1,0:T(8,128)} %copy-done.8) | copy-start | bytes 786436
  183.7 65.8 %all-reduce.21.cloned.1.call-start = ((), (), s32[]{:S(2)}) async-start(), calls=%async_computation.3 | async-start | bytes 524288 | tf_op jit(solution)/shard_map/psum | solution.py:128
  217.0 74.8 %all-reduce.23.cloned.1.call-start = ((), (), s32[]{:S(2)}) async-start(), calls=%async_computation.4 | async-start | bytes 2097152 | tf_op jit(solution)/shard_map/psum | solution.py:131
  292.8 6.3 %collective-permute-start.6 = (f32[128,1]{1,0:T(8,128)S(1)}, f32[128,1]{1,0:T(8,128)S(1)}, u32[]{:S(2)}, u32[]{:S(2)}) collective-permute-start(f32[128,1]{1,0:T(8,128)S(1)} %get-tuple-element.38), channel_id=1, source_target_pairs={{0,1},{1,2},{2,3},{3,4},{4,5},{5,6},{6,7},{8,9},{9,10},{10,11},{11... | collective-permute-start | bytes 1544 | tf_op jit(solution)/shard_map/ppermute | solution.py:18
  296.2 6.2 %collective-permute-start.7 = (f32[128,1]{1,0:T(8,128)S(1)}, f32[128,1]{1,0:T(8,128)S(1)}, u32[]{:S(2)}, u32[]{:S(2)}) collective-permute-start(f32[128,1]{1,0:T(8,128)S(1)} %get-tuple-element.39), channel_id=1, source_target_pairs={{1,0},{2,1},{3,2},{4,3},{5,4},{6,5},{7,6},{9,8},{10,9},{11,10},{12... | collective-permute-start | bytes 1544 | tf_op jit(solution)/shard_map/ppermute | solution.py:21
  (7 other events, 21.4 us)
Sparse Core Ops, SparseCore 0:
  23.1 35.6 all-reduce.14
  61.2 32.2 all-reduce.16
  99.4 36.4 all-reduce.24
  183.8 31.0 all-reduce.18
  217.1 32.2 all-reduce.20
  255.3 36.4 all-reduce.22
where the time goes:
time: 336 us; the launch traced here: 335 us
  waiting for transfers between devices  214 us (64%)
  blocking collectives  40.4 us (12%)
  other arithmetic  37 us (11%)
  starting transfers between devices  22.2 us (7%)
  between operations  17.1 us (5%)
  local copies, waits for them, and re-layouts  4.48 us (1%)
    psum x2, waiting for transfers between devices, shards(): lax.psum((grad_x, grad_y, grad_direct, grad_albedo), 'light')  73.2 us
    pmax x2, waiting for transfers between devices, shards(): highest = lax.pmax(local_high, 'light')  67 us
    psum x2, waiting for transfers between devices, shards(): summed = lax.psum(jnp.sum(raised, axis=0), 'light')  64.9 us
    psum x2, blocking collectives, shards(): lax.psum((jnp.sum(full_depth * full_depth), jnp.sum(full_albedo * full_al...  40.4 us
    ppermute x4, starting transfers between devices, extended(): lax.ppermute(lax.slice_in_dim(block, block.shape[dim] - width, None, axis...  16.8 us
    reduce_sum x2, other arithmetic, light_gradients(): grad_x = jnp.sum(scaled * (-delta_x - facing * slope_x / norm_sq), axis=0)  11.5 us
  transfers between devices with their start and end apart: 14, of which 11 were waited for; matrix products, arithmetic and copies ran while one was open for 2% of the time, Pallas kernels for 0%

commit v1 on v0

--- a/solution.py
+++ b/solution.py
@@ -8,6 +8,11 @@
 step_depth = 0.1
 step_albedo = 0.2
 epsilon = 1e-06
+
+
+def gather_and_add(x, mesh_axis):
+    pieces = lax.all_gather(x, mesh_axis)
+    return jnp.sum(pieces, axis=0)
 
 
 def extended(block, sides, width):
@@ -125,7 +130,7 @@
         local_high = jnp.max(scores, axis=0)
         highest = lax.pmax(local_high, "light")
         raised = jnp.exp(scores - highest)
-        summed = lax.psum(jnp.sum(raised, axis=0), "light")
+        summed = gather_and_add(jnp.sum(raised, axis=0), "light")
         weights = raised / summed
         grad_x, grad_y, grad_direct, grad_albedo = light_gradients(weights, terms, albedo)
         grad_x, grad_y, grad_direct, full_albedo = lax.psum(

time: 336 us -> 309 us (0.920)
  waiting for transfers between devices: 214 us -> 182 us
  other arithmetic: 37 us -> 41.3 us
    psum x2 -> x0, waiting for transfers between devices: 64.9 us -> none  [shards(): summed = lax.psum(jnp.sum(raised, axis=0), 'light')]
    all_gather x0 -> x2, waiting for transfers between devices: none -> 33.6 us  [gather_and_add(): pieces = lax.all_gather(x, mesh_axis)]
    reduce_sum x2 -> x4, other arithmetic: 4.16 us -> 8.39 us  [the longest x2 4.31 us: shards(): summed = gather_and_add(jnp.sum(raised, axis=0), 'light')]
where the time goes in v1:
time: 309 us; the launch traced here: 308 us
  waiting for transfers between devices  182 us (59%)
  other arithmetic  41.3 us (13%)
  blocking collectives  40.4 us (13%)
  starting transfers between devices  22.2 us (7%)
  between operations  17.1 us (6%)
  local copies, waits for them, and re-layouts  4.48 us (1%)
    psum x2, waiting for transfers between devices, shards(): lax.psum((grad_x, grad_y, grad_direct, grad_albedo), 'light')  73.1 us
    pmax x2, waiting for transfers between devices, shards(): highest = lax.pmax(local_high, 'light')  67 us
    psum x2, blocking collectives, shards(): lax.psum((jnp.sum(full_depth * full_depth), jnp.sum(full_albedo * full_al...  40.4 us
    all_gather x2, waiting for transfers between devices, gather_and_add(): pieces = lax.all_gather(x, mesh_axis)  33.6 us
    ppermute x4, starting transfers between devices, extended(): lax.ppermute(lax.slice_in_dim(block, block.shape[dim] - width, None, axis...  16.8 us
    reduce_sum x2, other arithmetic, light_gradients(): grad_x = jnp.sum(scaled * (-delta_x - facing * slope_x / norm_sq), axis=0)  11.5 us
    reduce_max x2, other arithmetic, shards(): local_high = jnp.max(scores, axis=0)  6.72 us
    ppermute x4, waiting for transfers between devices, extended(): lax.ppermute(lax.slice_in_dim(block, 0, width, axis=dim), axis, backward)  6.7 us
  transfers between devices with their start and end apart: 14, of which 11 were waited for; matrix products, arithmetic and copies ran while one was open for 2% of the time, Pallas kernels for 0%

profile of v1, /device:TPU:0, one launch (start us, length us, event | category | flops | bytes accessed | tf_op | source)
XLA Modules:
  0.0 307.8 jit_solution(5121574028369564770)
XLA Ops:
  9.6 5.5 %collective-permute-start.1 = (f32[128,1]{1,0:T(8,128)S(1)}, f32[128,1]{1,0:T(8,128)S(1)}, u32[]{:S(2)}, u32[]{:S(2)}) collective-permute-start(f32[128,1]{1,0:T(8,128)S(1)} %get-tuple-element.45), channel_id=1, source_target_pairs={{0,1},{1,2},{2,3},{3,4},{4,5},{5,6},{6,7},{8,9},{9,10},{10,11},{11... | collective-permute-start | bytes 1544 | tf_op jit(solution)/shard_map/ppermute | solution.py:23
  17.1 2.4 fusion.45
  20.3 2.7 fusion.15
  23.1 35.8 %all-reduce.13.cloned.1.call-done = f32[128,512]{1,0:T(8,128)} async-done(((f32[128,512]{1,0:T(8,128)}), f32[128,512]{1,0:T(8,128)}) %all-reduce.13.cloned.1.call-update) | async-done | bytes 262160 | tf_op jit(solution)/shard_map/pmax | solution.py:131
  58.9 2.2 fusion.14
  61.2 16.8 %all-gather.5.cloned.1.call-done = f32[512,512]{1,0:T(8,128)} async-done(((f32[128,512]{1,0:T(8,128)}), f32[512,512]{1,0:T(8,128)}) %all-gather.5.cloned.1.call-update) | async-done | bytes 1048592 | tf_op jit(solution)/shard_map/all_gather | solution.py:14
  78.0 2.1 reduce_sum.145
  80.0 5.8 %multiply_reduce_fusion.5 = (f32[128,512]{1,0:T(8,128)}, f32[128,512]{1,0:T(8,128)}, f32[128,512]{1,0:T(8,128)}, f32[128,512]{1,0:T(8,128)}) fusion(f32[128,512]{1,0:T(8,128)} %get-tuple-element.35, f32[128,512]{1,0:T(8,128)} %copy-done.15, f32[8,512]{1,0:T(8,128)S(1)} %get-tuple-element.46, f32[8,128]{1,0:T(8,128)S(1)} %get-tuple-element.55, ...), kind=kLoop, calls=%fused_computation.33 | loop fusion | flops 18612224 | bytes 5566528 | tf_op jit(solution)/shard_map/reduce_sum | solution.py:87
  85.9 36.5 %all-reduce.19.cloned.1.call-done = (f32[128,512]{1,0:T(8,128)}, f32[128,512]{1,0:T(8,128)}, f32[128,512]{1,0:T(8,128)}, f32[128,512]{1,0:T(8,128)}) async-done(((f32[128,512]{1,0:T(8,128)}, f32[128,512]{1,0:T(8,128)}, f32[128,512]{1,0:T(8,128)}, f32[128,512]{1,0:T(8,128)}), (f32[128,512]{1,0:T(8,128)}, f32[128,512]{1,0:T(8,128)}, f32[128,512]{1,0:T(8,128)}, ...) | async-done | bytes 1048592 | tf_op jit(solution)/shard_map/psum | solution.py:136
  123.4 3.4 %collective-permute-start.2 = (f32[128,1]{1,0:T(8,128)S(1)}, f32[128,1]{1,0:T(8,128)S(1)}, u32[]{:S(2)}, u32[]{:S(2)}) collective-permute-start(f32[128,1]{1,0:T(8,128)S(1)} %get-tuple-element.42), channel_id=1, source_target_pairs={{0,1},{1,2},{2,3},{3,4},{4,5},{5,6},{6,7},{8,9},{9,10},{10,11},{11... | collective-permute-start | bytes 1544 | tf_op jit(solution)/shard_map/ppermute | solution.py:23
  129.8 3.2 %collective-permute-done.3 = f32[128,1]{1,0:T(8,128)S(1)} collective-permute-done((f32[128,1]{1,0:T(8,128)S(1)}, f32[128,1]{1,0:T(8,128)S(1)}, u32[]{:S(2)}, u32[]{:S(2)}) %collective-permute-start.3) | collective-permute-done | bytes 544 | tf_op jit(solution)/shard_map/ppermute | solution.py:26
  133.0 2.1 multiply_reduce_fusion.9
  135.1 20.2 %all-reduce.5 = (f32[]{:T(128)}, f32[]{:T(128)}) all-reduce(f32[]{:T(128)} %get-tuple-element.30, f32[]{:T(128)} %multiply_reduce_fusion.8), channel_id=1, replica_groups=mesh['light'=4,'strip'=8] {'strip'}, use_global_device_ids=true, to_apply=%region_11.12 | all-reduce | flops 2 | bytes 16 | tf_op jit(solution)/shard_map/psum | solution.py:141
  158.2 4.5 %collective-permute-start.5 = (f32[128,1]{1,0:T(8,128)S(1)}, f32[128,1]{1,0:T(8,128)S(1)}, u32[]{:S(2)}, u32[]{:S(2)}) collective-permute-start(f32[128,1]{1,0:T(8,128)S(1)} %get-tuple-element.41), channel_id=1, source_target_pairs={{0,1},{1,2},{2,3},{3,4},{4,5},{5,6},{6,7},{8,9},{9,10},{10,11},{11... | collective-permute-start | bytes 1544 | tf_op jit(solution)/shard_map/ppermute | solution.py:23
  166.3 4.0 %fusion.17 = (f32[128,512]{1,0:T(8,128)}, f32[8,128,512]{2,1,0:T(8,128)S(1)}) fusion(bf16[8,128,512]{2,1,0:T(8,128)(2,1)} %param.7, f32[8,128]{1,0:T(8,128)S(1)} %get-tuple-element.55, f32[128,512]{1,0:T(8,128)S(1)} %get-tuple-element.29, f32[8,512]{1,0:T(8,128)S(1)} %get-tuple-element.48, f32[128,512]{1,0:T(8,128)S(1)} %neg.27, ...), kind=kLoop, calls=%fused_computation.41 | loop fusion | flops 9895936 | bytes 5021760 | tf_op jit(solution)/shard_map/reduce_max | solution.py:130
  170.3 31.2 %all-reduce.15.cloned.1.call-done = f32[128,512]{1,0:T(8,128)} async-done(((f32[128,512]{1,0:T(8,128)}), f32[128,512]{1,0:T(8,128)}) %all-reduce.15.cloned.1.call-update) | async-done | bytes 262160 | tf_op jit(solution)/shard_map/pmax | solution.py:131
  201.5 2.1 fusion.16
  203.7 16.8 %all-gather.7.cloned.1.call-done = f32[512,512]{1,0:T(8,128)} async-done(((f32[128,512]{1,0:T(8,128)}), f32[512,512]{1,0:T(8,128)}) %all-gather.7.cloned.1.call-update) | async-done | bytes 1048592 | tf_op jit(solution)/shard_map/all_gather | solution.py:14
  222.5 5.7 %multiply_reduce_fusion.2 = (f32[128,512]{1,0:T(8,128)}, f32[128,512]{1,0:T(8,128)}, f32[128,512]{1,0:T(8,128)}, f32[128,512]{1,0:T(8,128)}) fusion(f32[128,512]{1,0:T(8,128)} %get-tuple-element.27, f32[128,512]{1,0:T(8,128)} %copy-done.14, f32[128,512]{1,0:T(8,128)S(1)} %copy-done.9, f32[128,512]{1,0:T(8,128)S(1)} %neg.27, ...), kind=kLoop, calls=%fused_computation.28 | loop fusion | flops 18612224 | bytes 5566528 | tf_op jit(solution)/shard_map/reduce_sum | solution.py:87
  228.3 36.6 %all-reduce.17.cloned.1.call-done = (f32[128,512]{1,0:T(8,128)}, f32[128,512]{1,0:T(8,128)}, f32[128,512]{1,0:T(8,128)}, f32[128,512]{1,0:T(8,128)}) async-done(((f32[128,512]{1,0:T(8,128)}, f32[128,512]{1,0:T(8,128)}, f32[128,512]{1,0:T(8,128)}, f32[128,512]{1,0:T(8,128)}), (f32[128,512]{1,0:T(8,128)}, f32[128,512]{1,0:T(8,128)}, f32[128,512]{1,0:T(8,128)}, ...) | async-done | bytes 1048592 | tf_op jit(solution)/shard_map/psum | solution.py:136
  265.8 3.4 %collective-permute-start.6 = (f32[128,1]{1,0:T(8,128)S(1)}, f32[128,1]{1,0:T(8,128)S(1)}, u32[]{:S(2)}, u32[]{:S(2)}) collective-permute-start(f32[128,1]{1,0:T(8,128)S(1)} %get-tuple-element.38), channel_id=1, source_target_pairs={{0,1},{1,2},{2,3},{3,4},{4,5},{5,6},{6,7},{8,9},{9,10},{10,11},{11... | collective-permute-start | bytes 1544 | tf_op jit(solution)/shard_map/ppermute | solution.py:23
  272.2 3.2 %collective-permute-done.7 = f32[128,1]{1,0:T(8,128)S(1)} collective-permute-done((f32[128,1]{1,0:T(8,128)S(1)}, f32[128,1]{1,0:T(8,128)S(1)}, u32[]{:S(2)}, u32[]{:S(2)}) %collective-permute-start.7) | collective-permute-done | bytes 544 | tf_op jit(solution)/shard_map/ppermute | solution.py:26
  275.4 2.1 multiply_reduce_fusion.7
  277.5 20.2 %all-reduce.4 = (f32[]{:T(128)}, f32[]{:T(128)}) all-reduce(f32[]{:T(128)} %get-tuple-element.22, f32[]{:T(128)} %multiply_reduce_fusion.6), channel_id=1, replica_groups=mesh['light'=4,'strip'=8] {'strip'}, use_global_device_ids=true, to_apply=%region_27.28 | all-reduce | flops 2 | bytes 16 | tf_op jit(solution)/shard_map/psum | solution.py:141
  (76 shorter events, 22.0 us)
Async XLA Ops:
  7.2 13.1 %copy-start = (f32[128,512]{1,0:T(8,128)S(1)}, f32[128,512]{1,0:T(8,128)}, u32[]{:S(2)}) copy-start(f32[128,512]{1,0:T(8,128)} %param.5) | copy-start | bytes 786436
  7.2 13.1 %copy-start.1 = (bf16[8,128,512]{2,1,0:T(8,128)(2,1)S(1)}, bf16[8,128,512]{2,1,0:T(8,128)(2,1)}, u32[]{:S(2)}) copy-start(bf16[8,128,512]{2,1,0:T(8,128)(2,1)} %param.7) | copy-start | bytes 3145732
  7.2 51.7 %all-reduce.13.cloned.1.call-start = ((), (), s32[]{:S(2)}) async-start(), calls=%async_computation | async-start | bytes 524288 | tf_op jit(solution)/shard_map/pmax | solution.py:131
  8.3 8.7 %collective-permute-start = (f32[128,1]{1,0:T(8,128)S(1)}, f32[128,1]{1,0:T(8,128)S(1)}, u32[]{:S(2)}, u32[]{:S(2)}) collective-permute-start(f32[128,1]{1,0:T(8,128)S(1)} %get-tuple-element.44), channel_id=1, source_target_pairs={{1,0},{2,1},{3,2},{4,3},{5,4},{6,5},{7,6},{9,8},{10,9},{11,10},{12... | collective-permute-start | bytes 1544 | tf_op jit(solution)/shard_map/ppermute | solution.py:26
  9.6 7.6 %collective-permute-start.1 = (f32[128,1]{1,0:T(8,128)S(1)}, f32[128,1]{1,0:T(8,128)S(1)}, u32[]{:S(2)}, u32[]{:S(2)}) collective-permute-start(f32[128,1]{1,0:T(8,128)S(1)} %get-tuple-element.45), channel_id=1, source_target_pairs={{0,1},{1,2},{2,3},{3,4},{4,5},{5,6},{6,7},{8,9},{9,10},{10,11},{11... | collective-permute-start | bytes 1544 | tf_op jit(solution)/shard_map/ppermute | solution.py:23
  17.0 6.0 %copy-start.2 = (f32[128,512]{1,0:T(8,128)}, f32[128,512]{1,0:T(8,128)S(1)}, u32[]{:S(2)}) copy-start(f32[128,512]{1,0:T(8,128)S(1)} %convert_element_type.30) | copy-start | bytes 786436
  23.0 54.9 %all-gather.5.cloned.1.call-start = ((), (), s32[]{:S(2)}) async-start(), calls=%async_computation.2 | async-start | bytes 1310720 | tf_op jit(solution)/shard_map/all_gather | solution.py:14
  58.9 21.1 %copy-start.5 = (f32[128,512]{1,0:T(8,128)S(1)}, f32[128,512]{1,0:T(8,128)}, u32[]{:S(2)}) copy-start(f32[128,512]{1,0:T(8,128)} %copy-done.4) | copy-start | bytes 786436
  58.9 21.1 %copy-start.7 = (f32[128,512]{1,0:T(8,128)S(1)}, f32[128,512]{1,0:T(8,128)}, u32[]{:S(2)}) copy-start(f32[128,512]{1,0:T(8,128)} %param.6) | copy-start | bytes 786436
  58.9 21.1 %copy-start.11 = (f32[128,512]{1,0:T(8,128)S(1)}, f32[128,512]{1,0:T(8,128)}, u32[]{:S(2)}) copy-start(f32[128,512]{1,0:T(8,128)} %copy-done.10) | copy-start | bytes 786436
  58.9 21.1 %copy-start.13 = (f32[128,512]{1,0:T(8,128)S(1)}, f32[128,512]{1,0:T(8,128)}, u32[]{:S(2)}) copy-start(f32[128,512]{1,0:T(8,128)} %copy-done.12) | copy-start | bytes 786436
  61.1 61.3 %all-reduce.19.cloned.1.call-start = ((), (), s32[]{:S(2)}) async-start(), calls=%async_computation.5 | async-start | bytes 2097152 | tf_op jit(solution)/shard_map/psum | solution.py:136
  85.8 115.6 %all-reduce.15.cloned.1.call-start = ((), (), s32[]{:S(2)}) async-start(), calls=%async_computation.1 | async-start | bytes 524288 | tf_op jit(solution)/shard_map/pmax | solution.py:131
  122.4 40.3 %copy-start.16 = (f32[128,512]{1,0:T(8,128)S(1)}, f32[128,512]{1,0:T(8,128)}, u32[]{:S(2)}) copy-start(f32[128,512]{1,0:T(8,128)} %get-tuple-element.21) | copy-start | bytes 786436
  123.4 6.3 %collective-permute-start.2 = (f32[128,1]{1,0:T(8,128)S(1)}, f32[128,1]{1,0:T(8,128)S(1)}, u32[]{:S(2)}, u32[]{:S(2)}) collective-permute-start(f32[128,1]{1,0:T(8,128)S(1)} %get-tuple-element.42), channel_id=1, source_target_pairs={{0,1},{1,2},{2,3},{3,4},{4,5},{5,6},{6,7},{8,9},{9,10},{10,11},{11... | collective-permute-start | bytes 1544 | tf_op jit(solution)/shard_map/ppermute | solution.py:23
  126.8 6.2 %collective-permute-start.3 = (f32[128,1]{1,0:T(8,128)S(1)}, f32[128,1]{1,0:T(8,128)S(1)}, u32[]{:S(2)}, u32[]{:S(2)}) collective-permute-start(f32[128,1]{1,0:T(8,128)S(1)} %get-tuple-element.43), channel_id=1, source_target_pairs={{1,0},{2,1},{3,2},{4,3},{5,4},{6,5},{7,6},{9,8},{10,9},{11,10},{12... | collective-permute-start | bytes 1544 | tf_op jit(solution)/shard_map/ppermute | solution.py:26
  135.1 31.1 %copy-start.3 = (f32[128,512]{1,0:T(8,128)S(1)}, f32[128,512]{1,0:T(8,128)}, u32[]{:S(2)}) copy-start(f32[128,512]{1,0:T(8,128)} %copy-done.2) | copy-start | bytes 786436
  156.9 6.2 %collective-permute-start.4 = (f32[128,1]{1,0:T(8,128)S(1)}, f32[128,1]{1,0:T(8,128)S(1)}, u32[]{:S(2)}, u32[]{:S(2)}) collective-permute-start(f32[128,1]{1,0:T(8,128)S(1)} %get-tuple-element.40), channel_id=1, source_target_pairs={{1,0},{2,1},{3,2},{4,3},{5,4},{6,5},{7,6},{9,8},{10,9},{11,10},{12... | collective-permute-start | bytes 1544 | tf_op jit(solution)/shard_map/ppermute | solution.py:26
  158.2 6.4 %collective-permute-start.5 = (f32[128,1]{1,0:T(8,128)S(1)}, f32[128,1]{1,0:T(8,128)S(1)}, u32[]{:S(2)}, u32[]{:S(2)}) collective-permute-start(f32[128,1]{1,0:T(8,128)S(1)} %get-tuple-element.41), channel_id=1, source_target_pairs={{0,1},{1,2},{2,3},{3,4},{4,5},{5,6},{6,7},{8,9},{9,10},{10,11},{11... | collective-permute-start | bytes 1544 | tf_op jit(solution)/shard_map/ppermute | solution.py:23
  170.3 50.2 %all-gather.7.cloned.1.call-start = ((), (), s32[]{:S(2)}) async-start(), calls=%async_computation.3 | async-start | bytes 1310720 | tf_op jit(solution)/shard_map/all_gather | solution.py:14
  201.5 21.0 %copy-start.9 = (f32[128,512]{1,0:T(8,128)S(1)}, f32[128,512]{1,0:T(8,128)}, u32[]{:S(2)}) copy-start(f32[128,512]{1,0:T(8,128)} %copy-done.8) | copy-start | bytes 786436
  203.6 61.3 %all-reduce.17.cloned.1.call-start = ((), (), s32[]{:S(2)}) async-start(), calls=%async_computation.4 | async-start | bytes 2097152 | tf_op jit(solution)/shard_map/psum | solution.py:136
  265.8 6.3 %collective-permute-start.6 = (f32[128,1]{1,0:T(8,128)S(1)}, f32[128,1]{1,0:T(8,128)S(1)}, u32[]{:S(2)}, u32[]{:S(2)}) collective-permute-start(f32[128,1]{1,0:T(8,128)S(1)} %get-tuple-element.38), channel_id=1, source_target_pairs={{0,1},{1,2},{2,3},{3,4},{4,5},{5,6},{6,7},{8,9},{9,10},{10,11},{11... | collective-permute-start | bytes 1544 | tf_op jit(solution)/shard_map/ppermute | solution.py:23
  269.2 6.2 %collective-permute-start.7 = (f32[128,1]{1,0:T(8,128)S(1)}, f32[128,1]{1,0:T(8,128)S(1)}, u32[]{:S(2)}, u32[]{:S(2)}) collective-permute-start(f32[128,1]{1,0:T(8,128)S(1)} %get-tuple-element.39), channel_id=1, source_target_pairs={{1,0},{2,1},{3,2},{4,3},{5,4},{6,5},{7,6},{9,8},{10,9},{11,10},{12... | collective-permute-start | bytes 1544 | tf_op jit(solution)/shard_map/ppermute | solution.py:26
  (7 other events, 21.6 us)
Sparse Core Ops, SparseCore 0:
  23.2 35.6 all-reduce.12
  61.2 16.6 all-gather.4
  86.0 36.4 all-reduce.18
  170.4 31.0 all-reduce.14
  203.8 16.6 all-gather.6
  228.4 36.4 all-reduce.16
